TPU v7x, 512 devices: a whole 4x4x16 slice. The times are simulated.
512 devices in a mesh: led: 32 (over z, core), tile: 16 (over y, x).
Axes of the slice: x: 4, y: 4, z: 16, core: 2. Of those that a mesh axis runs over, the one named last changes fastest.
Arguments:
- spectrum: float32 [16, 8, 16, 32, 4096], P(None, None, 'tile', 'led'), may hold values from -6 to 6
- intensities: bfloat16 [32, 1024, 1024], P('led', 'tile'), may hold values from 0 to 2
- led_of_slot: int32 [32], replicated, may hold values from 0 to 31, each once
- row_offset: int32 [32], replicated, may hold values from 0 to 120
- col_offset: int32 [32], replicated, may hold values from 0 to 56
- tile_mask: int32 [32, 8, 8], replicated, may hold values 0 or 1
- aberration: float32 [5], replicated, may hold values from -1.5 to 1.5
Outputs:
- updated: float32 [16, 8, 16, 32, 4096], P(None, None, 'tile', 'led')
Inputs may be any that keep to these rules, and one draw needn't show every extreme that they name: `led_of_slot`: every LED is imaged in exactly one slot.
All inputs are finite; a program needn't handle non-finite values.
Results may differ from a plain program's by a relative error of at most 0.0003.
Values sent between devices are 32-bit elements; how exact they have to be, the bound alone decides.
A program may use at most 64 MiB of HBM per device.

v0:
```python
import math

import jax
import jax.numpy as jnp
import numpy as np
from jax import lax
from jax.experimental import pallas as pl
from jax.experimental.pallas import tpu as pltpu
from jax.sharding import PartitionSpec as P

M = 1024
TILE = 128
GR = 16
GC = 8
N_LED = 32
N_TILE = 16
BAND = M // N_TILE
CU = M // N_LED
LINES = BAND * CU // 128
STEP_SIZE = 0.25
MESH = pl.DeviceIdType.MESH


def turn(re, im, angle):
    eighth = round(angle / (math.pi / 4.0), 9)
    if eighth == int(eighth) and int(eighth) % 2 == 0:
        quarter = int(eighth) // 2 % 4
        return ((re, im), (-im, re), (-re, -im), (im, -re))[quarter]
    cos, sin = math.cos(angle), math.sin(angle)
    return re * cos - im * sin, im * cos + re * sin


def fft_points(parts, sign):
    count = len(parts)
    if count == 1:
        return list(parts)
    if count == 2:
        (ar, ai), (br, bi) = parts
        return [(ar + br, ai + bi), (ar - br, ai - bi)]
    quarter = count // 4
    subs = [fft_points(parts[r::4], sign) for r in range(4)]
    out = [None] * count
    for k in range(quarter):
        (ar, ai), (br, bi), (cr, ci), (dr, di) = (
            turn(*subs[r][k], sign * 2.0 * math.pi * r * k / count) for r in range(4)
        )
        sr, si, tr, ti = ar + cr, ai + ci, ar - cr, ai - ci
        ur, ui, vr, vi = br + dr, bi + di, br - dr, bi - di
        out[k] = (sr + ur, si + ui)
        out[k + 2 * quarter] = (sr - ur, si - ui)
        if sign > 0:
            out[k + quarter] = (tr - vi, ti + vr)
            out[k + 3 * quarter] = (tr + vi, ti - vr)
        else:
            out[k + quarter] = (tr + vi, ti - vr)
            out[k + 3 * quarter] = (tr - vi, ti + vr)
    return out


def digit(shape, axis, unit):
    return lax.broadcasted_iota(jnp.int32, shape, axis) // unit


def swapped(x, distance, axis):
    size = x.shape[axis]
    if 2 * distance == size:
        return pltpu.roll(x, distance, axis)
    low = digit(x.shape, axis, distance) % 2 == 0
    return jnp.where(low, pltpu.roll(x, size - distance, axis), pltpu.roll(x, distance, axis))


def four_forward(re, im, axis, unit):
    group = digit(re.shape, axis, unit)
    first = jnp.where(group < 2, 1.0, -1.0)
    second = jnp.where(group % 2 == 0, 1.0, -1.0)
    re = first * re + swapped(re, 2 * unit, axis)
    im = first * im + swapped(im, 2 * unit, axis)
    re, im = jnp.where(group == 3, -im, re), jnp.where(group == 3, re, im)
    return second * re + swapped(re, unit, axis), second * im + swapped(im, unit, axis)


def four_backward(re, im, axis, unit):
    group = digit(re.shape, axis, unit)
    first = jnp.where(group < 2, 1.0, -1.0)
    second = jnp.where(group % 2 == 0, 1.0, -1.0)
    re, im = second * re + swapped(re, unit, axis), second * im + swapped(im, unit, axis)
    re, im = jnp.where(group == 3, im, re), jnp.where(group == 3, -re, im)
    return first * re + swapped(re, 2 * unit, axis), first * im + swapped(im, 2 * unit, axis)


def cos_sin(phase):
    count = jnp.floor(phase * (2.0 / math.pi) + 0.5)
    rest = phase - count * 1.5703125
    rest = rest - count * 4.837512969970703125e-4
    rest = rest - count * 7.54978995489188216e-8
    square = rest * rest
    sin_rest = ((-1.9515295891e-4 * square + 8.3321608736e-3) * square - 1.6666654611e-1) * square * rest + rest
    cos_rest = (
        (2.443315711809948e-5 * square - 1.388731625493765e-3) * square + 4.166664568298827e-2
    ) * square * square - 0.5 * square + 1.0
    quadrant = count.astype(jnp.int32) & 3
    odd = (quadrant & 1) == 1
    cos = jnp.where(odd, sin_rest, cos_rest)
    sin = jnp.where(odd, cos_rest, sin_rest)
    cos = jnp.where((quadrant == 1) | (quadrant == 2), -cos, cos)
    return cos, jnp.where(quadrant >= 2, -sin, sin)


def halves(x):
    high = x.astype(jnp.bfloat16)
    return high, (x - high.astype(jnp.float32)).astype(jnp.bfloat16)


def product(left, right, dims):
    def one(a, b):
        return lax.dot_general(a, b, (dims, ((), ())), preferred_element_type=jnp.float32)

    return one(left[0], right[0]) + (one(left[0], right[1]) + one(left[1], right[0]))


def window_row(led_ref, row_ref, col_ref, slot, tile_here, led_here):
    led = led_ref[slot]
    row_start = row_ref[led] * TILE
    col_start = col_ref[led] * TILE
    row_group = (row_start + ((tile_here * BAND - row_start) & (M - 1))) >> 10
    col_group = (col_start + ((led_here * CU - col_start) & (M - 1))) >> 10
    return row_group * GC + col_group


def exchange_kernel(
    led_ref, row_ref, col_ref, mask_ref, aber_ref, spec_ref, image_ref, table_hi_ref, table_lo_ref,
    turn_u_ref, turn_j_ref, turn_h_ref, out_ref,
    outgoing, window, pupil, lines, lines_hi, lines_lo, bands_out, bands_in, cells, back_out, back_in,
    grad_out, grad_in, led_send, led_recv, tile_send, tile_recv, back_send, back_recv, grad_send, grad_recv,
):
    led_here = lax.axis_index("led")
    tile_here = lax.axis_index("tile")

    barrier = pltpu.get_barrier_semaphore()

    @pl.loop(1, N_LED)
    def _(step):
        pl.semaphore_signal(barrier, inc=1, device_id={"led": (led_here + step) % N_LED}, device_id_type=MESH)

    @pl.loop(1, N_TILE)
    def _(step):
        pl.semaphore_signal(barrier, inc=1, device_id={"tile": (tile_here + step) % N_TILE}, device_id_type=MESH)

    @pl.loop(0, N_LED)
    def _(slot):
        outgoing[slot] = spec_ref[window_row(led_ref, row_ref, col_ref, slot, tile_here, led_here)]

    def led_copy(src, dst, sends, recvs, peer):
        return pltpu.make_async_remote_copy(
            src_ref=src.at[peer], dst_ref=dst.at[led_here], send_sem=sends.at[peer], recv_sem=recvs.at[led_here],
            device_id={"led": peer}, device_id_type=MESH,
        )

    def led_arrival(src, dst, sends, recvs, peer):
        return pltpu.make_async_remote_copy(
            src_ref=src.at[peer], dst_ref=dst.at[peer], send_sem=sends.at[peer], recv_sem=recvs.at[peer],
            device_id={"led": peer}, device_id_type=MESH,
        )

    def tile_copy(src, dst, sends, recvs, peer):
        return pltpu.make_async_remote_copy(
            src_ref=src.at[peer], dst_ref=dst.at[tile_here], send_sem=sends.at[peer], recv_sem=recvs.at[tile_here],
            device_id={"tile": peer}, device_id_type=MESH,
        )

    def tile_arrival(src, dst, sends, recvs, peer):
        return pltpu.make_async_remote_copy(
            src_ref=src.at[peer], dst_ref=dst.at[peer], send_sem=sends.at[peer], recv_sem=recvs.at[peer],
            device_id={"tile": peer}, device_id_type=MESH,
        )

    def send_all(copy, count, here, *refs):
        @pl.loop(1, count)
        def _(step):
            ahead = (step + 1) // 2
            shift = jnp.where(step % 2 == 1, ahead, count - ahead)
            copy(*refs, (here + shift) % count).start()

    def wait_arrivals(arrival, count, here, *refs):
        @pl.loop(1, count)
        def _(step):
            arrival(*refs, (here + step) % count).wait_recv()

    def wait_sends(arrival, count, here, *refs):
        @pl.loop(1, count)
        def _(step):
            arrival(*refs, (here + step) % count).wait_send()

    pl.semaphore_wait(barrier, N_LED + N_TILE - 2)

    led_refs = (outgoing, window, led_send, led_recv)
    send_all(led_copy, N_LED, led_here, *led_refs)
    window[led_here] = outgoing[led_here]

    led = led_ref[led_here]
    row_start = row_ref[led] * TILE
    col_start = col_ref[led] * TILE
    lane = lax.broadcasted_iota(jnp.int32, (16, 128), 1)
    sub = lax.broadcasted_iota(jnp.int32, (16, 128), 0)
    row_first = (tile_here * BAND - row_start) & (M - 1)
    row_window = row_first + 4 * sub + lane // CU
    coord_p = (row_window - M // 2).astype(jnp.float32) * (1.0 / (M // 2))

    @pl.loop(0, N_LED)
    def _(part):
        col_first = (part * CU - col_start) & (M - 1)
        coord_q = (col_first + lane % CU - M // 2).astype(jnp.float32) * (1.0 / (M // 2))
        radial = coord_p * coord_p + coord_q * coord_q
        phase = (
            aber_ref[0] * (2.0 * radial - 1.0)
            + aber_ref[1] * (coord_p * coord_p - coord_q * coord_q)
            + aber_ref[2] * (2.0 * coord_p * coord_q)
            + aber_ref[3] * ((3.0 * radial - 2.0) * coord_p)
            + aber_ref[4] * ((3.0 * radial - 2.0) * coord_q)
        )
        gate = mask_ref[led * 64 + (row_first >> 7) * 8 + (col_first >> 7)].astype(jnp.float32)
        cos, sin = cos_sin(phase)
        pupil[0, part] = gate * cos
        pupil[1, part] = gate * sin

    wait_arrivals(led_arrival, N_LED, led_here, *led_refs)

    table = (table_hi_ref[...], table_lo_ref[...])

    @pl.loop(0, 2)
    def _(half):
        start = pl.multiple_of(half * 8, 8)
        parts = []
        for part in range(N_LED):
            pr, pi = pupil[0, part, pl.ds(start, 8)], pupil[1, part, pl.ds(start, 8)]
            wr, wi = window[part, pl.ds(start, 8)], window[part, pl.ds(16 + start, 8)]
            parts.append((pr * wr - pi * wi, pr * wi + pi * wr))
        for low, (re, im) in enumerate(fft_points(parts, 1.0)):
            cos, sin = turn_u_ref[0, pl.ds(low, 1)], turn_u_ref[1, pl.ds(low, 1)]
            lines[0, pl.ds(low * 16 + start, 8)] = re * cos - im * sin
            lines[1, pl.ds(low * 16 + start, 8)] = im * cos + re * sin

    @pl.loop(0, 16)
    def _(line):
        start = pl.multiple_of(line * 32, 32)
        for c in range(2):
            high, low = halves(lines[c, pl.ds(line, 32, stride=16)])
            lines_hi[pl.ds(start, 32), c * 128 : c * 128 + 128] = high
            lines_lo[pl.ds(start, 32), c * 128 : c * 128 + 128] = low

    bands_out[...] = product(table, (lines_hi[...], lines_lo[...]), ((1,), (1,))).reshape(16, 2, 8, 512)

    tile_refs = (bands_out, bands_in, tile_send, tile_recv)
    send_all(tile_copy, N_TILE, tile_here, *tile_refs)
    bands_in[tile_here] = bands_out[tile_here]
    wait_arrivals(tile_arrival, N_TILE, tile_here, *tile_refs)

    points = fft_points([(bands_in[k, 0], bands_in[k, 1]) for k in range(16)], 1.0)
    for low in range(16):
        re, im = points[low]
        quads = [
            turn(re[:, q * 128 : q * 128 + 128], im[:, q * 128 : q * 128 + 128], 2.0 * math.pi * low * q / 64)
            for q in range(4)
        ]
        for high, (qr, qi) in enumerate(fft_points(quads, 1.0)):
            cells[0, low + 16 * high] = qr
            cells[1, low + 16 * high] = qi

    @pl.loop(0, 8)
    def _(chunk):
        span = pl.ds(pl.multiple_of(chunk * 8, 8), 8)
        jr, ji = turn_j_ref[0, span], turn_j_ref[1, span]
        hr, hi = turn_h_ref[0][None], turn_h_ref[1][None]
        re, im = cells[0, span], cells[1, span]
        re, im = re * jr - im * ji, im * jr + re * ji
        re, im = four_forward(re, im, 2, 32)
        re, im = re * hr - im * hi, im * hr + re * hi
        re, im = four_forward(re, im, 1, 2)
        excess = re * re + im * im - image_ref[span]
        re, im = excess * re, excess * im
        re, im = four_backward(re, im, 1, 2)
        re, im = re * hr + im * hi, im * hr - re * hi
        re, im = four_backward(re, im, 2, 32)
        cells[0, span] = re * jr + im * ji
        cells[1, span] = im * jr - re * ji

    points = []
    for low in range(16):
        quads = fft_points([(cells[0, low + 16 * q], cells[1, low + 16 * q]) for q in range(4)], -1.0)
        quads = [turn(*quads[q], -2.0 * math.pi * low * q / 64) for q in range(4)]
        points.append(tuple(jnp.concatenate([quads[q][c] for q in range(4)], axis=1) for c in range(2)))
    for k, (re, im) in enumerate(fft_points(points, -1.0)):
        back_out[k, 0] = re
        back_out[k, 1] = im

    back_refs = (back_out, back_in, back_send, back_recv)
    send_all(tile_copy, N_TILE, tile_here, *back_refs)
    back_in[tile_here] = back_out[tile_here]
    wait_arrivals(tile_arrival, N_TILE, tile_here, *back_refs)

    mixed = product(halves(back_in[...].reshape(256, 512)), table, ((0,), (0,)))
    lines[0] = mixed[:, 0:128]
    lines[1] = mixed[:, 128:256]

    @pl.loop(0, 2)
    def _(half):
        start = pl.multiple_of(half * 8, 8)
        parts = []
        for low in range(N_LED):
            re, im = (lines[c, pl.ds(half * 256 + low, 8, stride=32)] for c in range(2))
            cos, sin = turn_u_ref[0, pl.ds(low, 1)], turn_u_ref[1, pl.ds(low, 1)]
            parts.append((re * cos + im * sin, im * cos - re * sin))
        for part, (re, im) in enumerate(fft_points(parts, -1.0)):
            pr, pi = pupil[0, part, pl.ds(start, 8)], pupil[1, part, pl.ds(start, 8)]
            grad_out[part, pl.ds(start, 8)] = pr * re + pi * im
            grad_out[part, pl.ds(16 + start, 8)] = pr * im - pi * re

    grad_refs = (grad_out, grad_in, grad_send, grad_recv)
    send_all(led_copy, N_LED, led_here, *grad_refs)
    grad_in[led_here] = grad_out[led_here]
    wait_arrivals(led_arrival, N_LED, led_here, *grad_refs)
    out_ref[...] = grad_in[...]

    wait_sends(led_arrival, N_LED, led_here, *led_refs)
    wait_sends(tile_arrival, N_TILE, tile_here, *tile_refs)
    wait_sends(tile_arrival, N_TILE, tile_here, *back_refs)
    wait_sends(led_arrival, N_LED, led_here, *grad_refs)


def update_kernel(led_ref, row_ref, col_ref, spec_ref, grad_ref, out_ref):
    led_here = lax.axis_index("led")
    tile_here = lax.axis_index("tile")
    out_ref[...] = spec_ref[...]

    @pl.loop(0, N_LED)
    def _(slot):
        row = window_row(led_ref, row_ref, col_ref, slot, tile_here, led_here)
        out_ref[row] = out_ref[row] - STEP_SIZE * grad_ref[slot]


def dft_tables():
    rank = np.arange(256)
    out_re = (rank // 8) % 2
    out_b = 2 * (rank // 16) + rank % 2
    out_j = (rank // 2) % 4
    in_re = rank // 128
    in_j = (rank // 32) % 4
    in_u = rank % 32
    angle = 2.0 * np.pi * ((out_b[:, None] * in_u[None, :]) % 32) / 32.0
    same = out_j[:, None] == in_j[None, :]
    real = np.where(
        out_re[:, None] == in_re[None, :], np.cos(angle), np.where(out_re[:, None] == 0, -np.sin(angle), np.sin(angle))
    )
    table = (same * real / M).astype(np.float32)
    table_hi = table.astype(jnp.bfloat16)
    table_lo = (table - table_hi.astype(np.float32)).astype(jnp.bfloat16)
    lane = np.arange(128)

    def turns(product, modulus):
        angle = 2.0 * np.pi * (product % modulus) / modulus
        return np.stack([np.cos(angle), np.sin(angle)]).astype(np.float32)

    turn_u = turns(np.arange(32)[:, None] * (lane % 32)[None, :], M)
    sub_j = np.arange(8) // 2
    turn_j = turns(np.arange(64)[:, None, None] * (4 * (lane // 32)[None, None, :] + sub_j[None, :, None]), M)
    frequency = np.array([0, 2, 1, 3])
    turn_h = turns(sub_j[:, None] * frequency[lane // 32][None, :], 16)
    return table_hi, table_lo, turn_u, turn_j, turn_h


def arrange_image(image):
    order = np.array([0, 2, 1, 3])
    cut = image.reshape(2, 32, 4, 4, 64)[:, :, order][:, :, :, order]
    return jnp.transpose(cut, (4, 2, 0, 3, 1)).reshape(64, 8, 128)


def shards(spectrum, intensities, led_of_slot, row_offset, col_offset, tile_mask, aberration):
    rows = spectrum.reshape(GR * GC, LINES * 2, 128)
    image = arrange_image(intensities.reshape(BAND, M)).astype(jnp.float32)
    table_hi, table_lo, turn_u, turn_j, turn_h = (jnp.asarray(t) for t in dft_tables())
    smem = pl.BlockSpec(memory_space=pltpu.SMEM)
    vmem = pl.BlockSpec(memory_space=pltpu.VMEM)
    message = pltpu.VMEM((N_LED, 32, 128), jnp.float32)
    band = pltpu.VMEM((N_TILE, 2, 8, 512), jnp.float32)
    leds = pltpu.SemaphoreType.DMA((N_LED,))
    tiles = pltpu.SemaphoreType.DMA((N_TILE,))
    grad = pl.pallas_call(
        exchange_kernel,
        out_shape=jax.ShapeDtypeStruct((N_LED, 32, 128), jnp.float32),
        in_specs=[smem] * 5 + [vmem] * 7,
        out_specs=vmem,
        scratch_shapes=[
            message,
            message,
            pltpu.VMEM((2, N_LED, 16, 128), jnp.float32),
            pltpu.VMEM((2, 512, 128), jnp.float32),
            pltpu.VMEM((512, 256), jnp.bfloat16),
            pltpu.VMEM((512, 256), jnp.bfloat16),
            band,
            band,
            pltpu.VMEM((2, 64, 8, 128), jnp.float32),
            band,
            band,
            message,
            message,
            leds,
            leds,
            tiles,
            tiles,
            tiles,
            tiles,
            leds,
            leds,
        ],
        compiler_params=pltpu.CompilerParams(
            collective_id=0, has_side_effects=True, vmem_limit_bytes=40 * 1024 * 1024
        ),
    )(
        led_of_slot, row_offset, col_offset, tile_mask.reshape(-1), aberration, rows, image,
        table_hi, table_lo, turn_u, turn_j, turn_h,
    )
    updated = pl.pallas_call(
        update_kernel,
        out_shape=jax.ShapeDtypeStruct((GR * GC, LINES * 2, 128), jnp.float32),
        in_specs=[smem] * 3 + [vmem] * 2,
        out_specs=vmem,
        compiler_params=pltpu.CompilerParams(vmem_limit_bytes=24 * 1024 * 1024),
    )(led_of_slot, row_offset, col_offset, rows, grad)
    return updated.reshape(spectrum.shape)


def solution(mesh):
    placed = (P(None, None, "tile", "led", None), P("led", "tile", None), P(), P(), P(), P(), P())
    return jax.shard_map(
        shards,
        mesh=mesh,
        in_specs=placed,
        out_specs=P(None, None, "tile", "led", None),
        check_vma=False,
    )
```

profile of v0, /device:TPU:1, one launch (start us, length us, event | category | flops | bytes accessed | tf_op | source)
XLA Modules:
  0.0 106.0 jit_solution(7370692420294115298)
XLA Ops:
  0.0 0.7 pad_clamp_fusion
  0.7 0.9 copy.26
  1.5 0.1 reshape.13.mask_ref
  1.6 1.1 %reshape_reshape.3 = bf16[2,32,4,4,64]{4,3,2,1,0:T(4,128)(2,1)S(1)} reshape(bf16[1,64,1024]{2,1,0:T(8,128)(2,1)} %param.16) | data formatting | bytes 262144 | tf_op jit(solution)/shard_map/reshape;reshape | solution.py:373
  2.8 0.1 copy.27
  2.8 0.0 copy-start
  2.9 0.0 copy-start.1
  2.9 0.0 copy-start.2
  2.9 0.0 copy-start.3
  2.9 0.0 copy-start.4
  2.9 0.0 copy-start.5
  2.9 0.0 copy-start.6
  2.9 0.0 copy-start.7
  2.9 0.0 copy-start.8
  3.0 0.0 copy-start.9
  3.0 1.3 %gather_fusion = bf16[4,2,32,4,64]{4,2,3,1,0:T(8,128)(2,1)} fusion(bf16[2,32,4,4,64]{4,1,3,2,0:T(8,128)(2,1)S(1)} %copy.27, s32[1024]{0:T(1024)S(1)} %pad_clamp_fusion), kind=kCustom, calls=%fused_computation | custom fusion | bytes 262160 | tf_op jit(solution)/shard_map/gather | solution.py:373
  4.2 1.0 copy.28
  5.2 0.6 gather_fusion.1
  5.8 0.1 convert_bitcast_fusion
  5.9 0.8 copy.29
  6.7 1.2 %copy.30.image_ref = f32[64,8,128]{2,1,0:T(8,128)S(1)} copy(f32[64,8,128]{0,2,1:T(8,128)} %bitcast.8) | data formatting | bytes 524288 | tf_op jit(solution)/shard_map/convert_element_type | solution.py:379
  8.0 0.0 copy-done
  8.0 0.0 copy-done.1
  8.0 0.0 copy-done.2
  8.0 0.0 copy-done.3
  8.0 0.0 copy-done.4
  8.0 0.0 copy-done.5
  8.0 0.0 copy-done.6
  8.0 0.0 copy-done.7
  8.1 0.0 copy-done.8
  8.1 95.5 %shard_map.145.grad_ref = f32[32,32,128]{2,1,0:T(8,128)S(1)} custom-call(s32[32]{0:T(128)S(1)} %copy-done.6, s32[32]{0:T(128)S(1)} %copy-done.7, s32[32]{0:T(128)S(1)} %copy-done.8, s32[2048]{0:T(1024)S(1)} %reshape.13.mask_ref, f32[5]{0:T(128)S(1)} %copy-done.9, f32[128,32,128]{2,1,0:T(8,128)S(1)} %bitcast.6, f32[64,8,128]{2,1,0:T(8,128)S(1)} %copy.30.image_ref, ...), custom_call_target="tpu_custom_call" | custom-call | tf_op jit(solution)/shard_map/pallas_call | solution.py:387
  103.6 2.5 %shard_map.146 = f32[128,32,128]{2,1,0:T(8,128)} custom-call(s32[32]{0:T(128)S(1)} %copy-done.6, s32[32]{0:T(128)S(1)} %copy-done.7, s32[32]{0:T(128)S(1)} %copy-done.8, f32[128,32,128]{2,1,0:T(8,128)S(1)} %bitcast.7, f32[32,32,128]{2,1,0:T(8,128)S(1)} %shard_map.145.grad_ref), custom_call_target="tpu_custom_call" | custom-call | tf_op jit(solution)/shard_map/pallas_call | solution.py:422
  (1 shorter events, 0.0 us)
Async XLA Ops:
  2.8 5.1 %copy-start = (f32[16,8,1,1,4096]{4,3,2,1,0:T(1,128)S(1)}, f32[16,8,1,1,4096]{4,3,2,1,0:T(1,128)}, u32[]{:S(2)}) copy-start(f32[16,8,1,1,4096]{4,3,2,1,0:T(1,128)} %param.15) | copy-start | bytes 6291460
  2.9 5.1 %copy-start.1 = (f32[2,64,8,128]{3,2,1,0:T(8,128)S(1)}, f32[2,64,8,128]{3,2,1,0:T(8,128)}, u32[]{:S(2)}) copy-start(f32[2,64,8,128]{3,2,1,0:T(8,128)} %constant.21.clone.turn_j_ref) | copy-start | bytes 1572868
  2.9 5.1 %copy-start.2 = (bf16[256,256]{1,0:T(8,128)(2,1)S(1)}, bf16[256,256]{1,0:T(8,128)(2,1)}, u32[]{:S(2)}) copy-start(bf16[256,256]{1,0:T(8,128)(2,1)} %constant.19.clone.table_lo_ref) | copy-start | bytes 393220
  2.9 5.1 %copy-start.3 = (bf16[256,256]{1,0:T(8,128)(2,1)S(1)}, bf16[256,256]{1,0:T(8,128)(2,1)}, u32[]{:S(2)}) copy-start(bf16[256,256]{1,0:T(8,128)(2,1)} %constant.18.clone.table_hi_ref) | copy-start | bytes 393220
  2.9 5.1 %copy-start.4 = (f32[2,32,128]{2,1,0:T(8,128)S(1)}, f32[2,32,128]{2,1,0:T(8,128)}, u32[]{:S(2)}) copy-start(f32[2,32,128]{2,1,0:T(8,128)} %constant.20.clone.turn_u_ref) | copy-start | bytes 98308
  2.9 5.1 %copy-start.5 = (f32[2,8,128]{2,1,0:T(8,128)S(1)}, f32[2,8,128]{2,1,0:T(8,128)}, u32[]{:S(2)}) copy-start(f32[2,8,128]{2,1,0:T(8,128)} %constant.22.clone.turn_h_ref) | copy-start | bytes 24580
  2.9 5.1 %copy-start.6 = (s32[32]{0:T(128)S(1)}, s32[32]{0:T(128)}, u32[]{:S(2)}) copy-start(s32[32]{0:T(128)} %led_ref.3) | copy-start | bytes 388
  2.9 5.1 %copy-start.7 = (s32[32]{0:T(128)S(1)}, s32[32]{0:T(128)}, u32[]{:S(2)}) copy-start(s32[32]{0:T(128)} %row_ref.3) | copy-start | bytes 388
  2.9 5.1 %copy-start.8 = (s32[32]{0:T(128)S(1)}, s32[32]{0:T(128)}, u32[]{:S(2)}) copy-start(s32[32]{0:T(128)} %col_ref.3) | copy-start | bytes 388
  3.0 5.1 %copy-start.9 = (f32[5]{0:T(128)S(1)}, f32[5]{0:T(128)}, u32[]{:S(2)}) copy-start(f32[5]{0:T(128)} %aber_ref.1) | copy-start | bytes 64
where the time goes:
time: 106 us
  Pallas kernels  97.9 us (92%)
  local copies, waits for them, and re-layouts  7.15 us (7%)
    pallas_call x1, Pallas kernels, shards(): pl.pallas_call(exchange_kernel, out_shape=jax.ShapeDtypeStruct((N_LED, 32...  95.5 us
    gather x3, local copies, waits for them, and re-layouts, arrange_image(): cut = image.reshape(2, 32, 4, 4, 64)[:, :, order][:, :, :, order]  2.85 us
    pallas_call x1, Pallas kernels, shards(): pl.pallas_call(update_kernel, out_shape=jax.ShapeDtypeStruct((GR * GC, LI...  2.46 us

commit v1 on v0

v1 whole, which is shorter than its diff:
```python
import math

import jax
import jax.numpy as jnp
from jax import lax
from jax.experimental import pallas as pl
from jax.experimental.pallas import tpu as pltpu
from jax.sharding import PartitionSpec as P

M = 1024
TILE = 128
GR = 16
GC = 8
N_LED = 32
N_TILE = 16
BAND = M // N_TILE
CU = M // N_LED
LINES = BAND * CU // 128
STEP_SIZE = 0.25
MESH = pl.DeviceIdType.MESH


def turn(re, im, angle):
    eighth = round(angle / (math.pi / 4.0), 9)
    if eighth == int(eighth) and int(eighth) % 2 == 0:
        quarter = int(eighth) // 2 % 4
        return ((re, im), (-im, re), (-re, -im), (im, -re))[quarter]
    cos, sin = math.cos(angle), math.sin(angle)
    return re * cos - im * sin, im * cos + re * sin


def fft_points(parts, sign):
    count = len(parts)
    if count == 1:
        return list(parts)
    if count == 2:
        (ar, ai), (br, bi) = parts
        return [(ar + br, ai + bi), (ar - br, ai - bi)]
    quarter = count // 4
    subs = [fft_points(parts[r::4], sign) for r in range(4)]
    out = [None] * count
    for k in range(quarter):
        (ar, ai), (br, bi), (cr, ci), (dr, di) = (
            turn(*subs[r][k], sign * 2.0 * math.pi * r * k / count) for r in range(4)
        )
        sr, si, tr, ti = ar + cr, ai + ci, ar - cr, ai - ci
        ur, ui, vr, vi = br + dr, bi + di, br - dr, bi - di
        out[k] = (sr + ur, si + ui)
        out[k + 2 * quarter] = (sr - ur, si - ui)
        if sign > 0:
            out[k + quarter] = (tr - vi, ti + vr)
            out[k + 3 * quarter] = (tr + vi, ti - vr)
        else:
            out[k + quarter] = (tr + vi, ti - vr)
            out[k + 3 * quarter] = (tr - vi, ti + vr)
    return out


def digit(shape, axis, unit):
    return lax.broadcasted_iota(jnp.int32, shape, axis) // unit


def swapped(x, distance, axis):
    size = x.shape[axis]
    if 2 * distance == size:
        return pltpu.roll(x, distance, axis)
    low = digit(x.shape, axis, distance) % 2 == 0
    return jnp.where(low, pltpu.roll(x, size - distance, axis), pltpu.roll(x, distance, axis))


def four_forward(re, im, axis, unit):
    group = digit(re.shape, axis, unit)
    first = jnp.where(group < 2, 1.0, -1.0)
    second = jnp.where(group % 2 == 0, 1.0, -1.0)
    re = first * re + swapped(re, 2 * unit, axis)
    im = first * im + swapped(im, 2 * unit, axis)
    re, im = jnp.where(group == 3, -im, re), jnp.where(group == 3, re, im)
    return second * re + swapped(re, unit, axis), second * im + swapped(im, unit, axis)


def four_backward(re, im, axis, unit):
    group = digit(re.shape, axis, unit)
    first = jnp.where(group < 2, 1.0, -1.0)
    second = jnp.where(group % 2 == 0, 1.0, -1.0)
    re, im = second * re + swapped(re, unit, axis), second * im + swapped(im, unit, axis)
    re, im = jnp.where(group == 3, im, re), jnp.where(group == 3, -re, im)
    return first * re + swapped(re, 2 * unit, axis), first * im + swapped(im, 2 * unit, axis)


def cos_sin(phase):
    count = jnp.floor(phase * (2.0 / math.pi) + 0.5)
    rest = phase - count * 1.5703125
    rest = rest - count * 4.837512969970703125e-4
    rest = rest - count * 7.54978995489188216e-8
    square = rest * rest
    sin_rest = ((-1.9515295891e-4 * square + 8.3321608736e-3) * square - 1.6666654611e-1) * square * rest + rest
    cos_rest = (
        (2.443315711809948e-5 * square - 1.388731625493765e-3) * square + 4.166664568298827e-2
    ) * square * square - 0.5 * square + 1.0
    quadrant = count.astype(jnp.int32) & 3
    odd = (quadrant & 1) == 1
    cos = jnp.where(odd, sin_rest, cos_rest)
    sin = jnp.where(odd, cos_rest, sin_rest)
    cos = jnp.where((quadrant == 1) | (quadrant == 2), -cos, cos)
    return cos, jnp.where(quadrant >= 2, -sin, sin)


def halves(x):
    high = x.astype(jnp.bfloat16)
    return high, (x - high.astype(jnp.float32)).astype(jnp.bfloat16)


def product(left, right, dims):
    def one(a, b):
        return lax.dot_general(a, b, (dims, ((), ())), preferred_element_type=jnp.float32)

    return one(left[0], right[0]) + (one(left[0], right[1]) + one(left[1], right[0]))


def window_row(led_ref, row_ref, col_ref, slot, tile_here, led_here):
    led = led_ref[slot]
    row_start = row_ref[led] * TILE
    col_start = col_ref[led] * TILE
    row_group = (row_start + ((tile_here * BAND - row_start) & (M - 1))) >> 10
    col_group = (col_start + ((led_here * CU - col_start) & (M - 1))) >> 10
    return row_group * GC + col_group


def exchange_kernel(
    led_ref, row_ref, col_ref, mask_ref, aber_ref, spec_hbm, image_hbm, out_ref,
    spec, measured, image, table_hi, table_lo, turn_u, turn_j,
    outgoing, window, pupil, lines, lines_hi, lines_lo, bands_out, bands_in, cells, back_out, back_in,
    grad_out, grad_in, spec_sem, image_sem,
    led_send, led_recv, tile_send, tile_recv, back_send, back_recv, grad_send, grad_recv,
):
    led_here = lax.axis_index("led")
    tile_here = lax.axis_index("tile")

    spec_copy = pltpu.make_async_copy(spec_hbm, spec, spec_sem)
    image_copy = pltpu.make_async_copy(image_hbm, measured, image_sem)
    spec_copy.start()
    image_copy.start()
    barrier = pltpu.get_barrier_semaphore()

    def far_first(step, count, here):
        away = step // 2
        return (here + count // 2 + jnp.where(step % 2 == 1, away, -away)) % count

    @pl.loop(1, N_LED)
    def _(step):
        peer = far_first(step, N_LED, led_here)
        pl.semaphore_signal(barrier, inc=1, device_id={"led": peer}, device_id_type=MESH)

    @pl.loop(1, N_TILE)
    def _(step):
        peer = far_first(step, N_TILE, tile_here)
        pl.semaphore_signal(barrier, inc=1, device_id={"tile": peer}, device_id_type=MESH)

    def led_copy(src, dst, sends, recvs, half, peer, origin):
        return pltpu.make_async_remote_copy(
            src_ref=src.at[half, peer], dst_ref=dst.at[half, origin],
            send_sem=sends.at[half, peer], recv_sem=recvs.at[half, origin],
            device_id={"led": peer}, device_id_type=MESH,
        )

    def tile_copy(src, dst, sends, recvs, half, peer, origin):
        return pltpu.make_async_remote_copy(
            src_ref=src.at[half, peer], dst_ref=dst.at[half, origin],
            send_sem=sends.at[half, peer], recv_sem=recvs.at[half, origin],
            device_id={"tile": peer}, device_id_type=MESH,
        )

    led_axis = (led_copy, N_LED, led_here)
    tile_axis = (tile_copy, N_TILE, tile_here)

    def send_half(axis, half, src, dst, sends, recvs):
        copy, count, here = axis

        @pl.loop(1, count)
        def _(step):
            copy(src, dst, sends, recvs, half, far_first(step, count, here), here).start()

        dst[half, here] = src[half, here]

    def wait_half(axis, half, src, dst, sends, recvs):
        copy, count, here = axis

        @pl.loop(1, count)
        def _(step):
            peer = far_first(step, count, here)
            copy(src, dst, sends, recvs, half, peer, peer).wait_recv()

    def wait_sent(axis, src, dst, sends, recvs):
        copy, count, here = axis

        @pl.loop(1, count)
        def _(step):
            peer = far_first(step, count, here)
            copy(src, dst, sends, recvs, 0, peer, peer).wait_send()
            copy(src, dst, sends, recvs, 1, peer, peer).wait_send()

    spec_copy.wait()

    @pl.loop(0, N_LED)
    def _(slot):
        row = window_row(led_ref, row_ref, col_ref, slot, tile_here, led_here)
        for half in range(2):
            for c in range(2):
                outgoing[half, slot, c] = spec[row, c * 16 + half * 8 : c * 16 + half * 8 + 8]

    def turns(index, modulus):
        return cos_sin((index & (modulus - 1)).astype(jnp.float32) * (2.0 * math.pi / modulus))

    def iota(shape, axis):
        return lax.broadcasted_iota(jnp.int32, shape, axis)

    @pl.loop(0, 8)
    def _(chunk):
        start = pl.multiple_of(chunk * 32, 32)
        rank = start + iota((32, 256), 0)
        entry = iota((32, 256), 1)
        cos, sin = turns((2 * (rank >> 4) + (rank & 1)) * (entry & 31), 32)
        out_im, in_im = (rank >> 3) & 1, entry >> 7
        value = jnp.where(out_im == in_im, cos, jnp.where(out_im == 0, -sin, sin))
        value = jnp.where(((rank >> 1) & 3) == ((entry >> 5) & 3), value * (1.0 / M), 0.0)
        high, low = halves(value)
        table_hi[pl.ds(start, 32), :] = high
        table_lo[pl.ds(start, 32), :] = low

    lane8 = iota((8, 128), 1)
    sub8 = iota((8, 128), 0)
    turn_u[0], turn_u[1] = turns(iota((32, 128), 0) * (iota((32, 128), 1) & 31), M)

    @pl.loop(0, 64)
    def _(low):
        turn_j[0, low], turn_j[1, low] = turns(low * (4 * (lane8 >> 5) + (sub8 >> 1)), M)

    chunk8 = lane8 >> 5
    frequency8 = jnp.where(chunk8 == 1, 2, jnp.where(chunk8 == 2, 1, chunk8))
    turn_hr, turn_hi = turns((sub8 >> 1) * frequency8, 16)

    led = led_ref[led_here]
    row_start = row_ref[led] * TILE
    col_start = col_ref[led] * TILE
    lane = iota((16, 128), 1)
    row_first = (tile_here * BAND - row_start) & (M - 1)
    row_window = row_first + 4 * iota((16, 128), 0) + (lane >> 5)
    coord_p = (row_window - M // 2).astype(jnp.float32) * (1.0 / (M // 2))

    @pl.loop(0, N_LED)
    def _(part):
        col_first = (part * CU - col_start) & (M - 1)
        coord_q = (col_first + (lane & 31) - M // 2).astype(jnp.float32) * (1.0 / (M // 2))
        radial = coord_p * coord_p + coord_q * coord_q
        phase = (
            aber_ref[0] * (2.0 * radial - 1.0)
            + aber_ref[1] * (coord_p * coord_p - coord_q * coord_q)
            + aber_ref[2] * (2.0 * coord_p * coord_q)
            + aber_ref[3] * ((3.0 * radial - 2.0) * coord_p)
            + aber_ref[4] * ((3.0 * radial - 2.0) * coord_q)
        )
        gate = mask_ref[(row_first >> 7) * 8 + (col_first >> 7), led].astype(jnp.float32)
        cos, sin = cos_sin(phase)
        pupil[0, part] = gate * cos
        pupil[1, part] = gate * sin

    pl.semaphore_wait(barrier, N_LED + N_TILE - 2)

    led_refs = (outgoing, window, led_send, led_recv)
    send_half(led_axis, 0, *led_refs)
    send_half(led_axis, 1, *led_refs)

    image_copy.wait()
    chunk64 = iota((64, 128), 1) >> 5
    for h in range(4):
        pieces = []
        for block in (2 * h, 2 * h + 1):
            lines_here = measured[0, :, block * 128 : block * 128 + 128].astype(jnp.float32)
            turned = jnp.transpose(jnp.concatenate([lines_here, lines_here], axis=0))
            rolled = pltpu.roll(turned, 32, 1)
            pieces += [(turned[f : f + 64], rolled[f : f + 64]) for f in (0, 64)]
        for s in range(2):
            merged = pieces[0][s]
            for m, f in ((1, 2), (2, 1), (3, 3)):
                merged = jnp.where(chunk64 == m, pieces[f][(m + s) % 2], merged)
            image[pl.ds((0, 2, 1, 3)[h] * 2 + s, 64, stride=8), :] = merged

    tile_refs = (bands_out, bands_in, tile_send, tile_recv)
    table = (table_hi[...], table_lo[...])
    for half in range(2):
        wait_half(led_axis, half, *led_refs)
        parts = []
        for part in range(N_LED):
            pr, pi = (pupil[c, part, half * 8 : half * 8 + 8] for c in range(2))
            wr, wi = window[half, part, 0], window[half, part, 1]
            parts.append((pr * wr - pi * wi, pr * wi + pi * wr))
        for low, (re, im) in enumerate(fft_points(parts, 1.0)):
            cos, sin = turn_u[0, low : low + 1], turn_u[1, low : low + 1]
            lines[0, low * 8 : low * 8 + 8] = re * cos - im * sin
            lines[1, low * 8 : low * 8 + 8] = im * cos + re * sin
        for line in range(8):
            for c in range(2):
                high, low = halves(lines[c, pl.ds(line, 32, stride=8)])
                lines_hi[line * 32 : line * 32 + 32, c * 128 : c * 128 + 128] = high
                lines_lo[line * 32 : line * 32 + 32, c * 128 : c * 128 + 128] = low
        mixed = product(table, (lines_hi[...], lines_lo[...]), ((1,), (1,)))
        bands_out[half] = mixed.reshape(N_TILE, 2, 8, 256)
        send_half(tile_axis, half, *tile_refs)

    for half in range(2):
        wait_half(tile_axis, half, *tile_refs)
        points = fft_points([(bands_in[half, k, 0], bands_in[half, k, 1]) for k in range(N_TILE)], 1.0)
        for low, (re, im) in enumerate(points):
            for side in range(2):
                q = 2 * half + side
                span = slice(side * 128, side * 128 + 128)
                cells[0, q, low], cells[1, q, low] = turn(re[:, span], im[:, span], 2.0 * math.pi * low * q / 64)

    @pl.loop(0, 4)
    def _(chunk):
        span = pl.ds(chunk * 4, 4)
        quads = fft_points([(cells[0, q, span], cells[1, q, span]) for q in range(4)], 1.0)
        back = []
        for q, (re, im) in enumerate(quads):
            where = pl.ds(16 * q + chunk * 4, 4)
            jr, ji = turn_j[0, where], turn_j[1, where]
            hr, hi = turn_hr[None], turn_hi[None]
            re, im = re * jr - im * ji, im * jr + re * ji
            re, im = four_forward(re, im, 2, 32)
            re, im = re * hr - im * hi, im * hr + re * hi
            re, im = four_forward(re, im, 1, 2)
            seen = image[pl.ds(pl.multiple_of((16 * q + chunk * 4) * 8, 32), 32), :].reshape(4, 8, 128)
            excess = re * re + im * im - seen
            re, im = excess * re, excess * im
            re, im = four_backward(re, im, 1, 2)
            re, im = re * hr + im * hi, im * hr - re * hi
            re, im = four_backward(re, im, 2, 32)
            back.append((re * jr + im * ji, im * jr - re * ji))
        for q, (re, im) in enumerate(fft_points(back, -1.0)):
            cells[0, q, span] = re
            cells[1, q, span] = im

    back_refs = (back_out, back_in, back_send, back_recv)
    for half in range(2):
        for side in range(2):
            q = 2 * half + side
            points = [turn(cells[0, q, low], cells[1, q, low], -2.0 * math.pi * low * q / 64) for low in range(16)]
            for k, (re, im) in enumerate(fft_points(points, -1.0)):
                back_out[half, k, 0, :, side * 128 : side * 128 + 128] = re
                back_out[half, k, 1, :, side * 128 : side * 128 + 128] = im
        send_half(tile_axis, half, *back_refs)

    grad_refs = (grad_out, grad_in, grad_send, grad_recv)
    for half in range(2):
        wait_half(tile_axis, half, *back_refs)
        mixed = product(halves(back_in[half].reshape(256, 256)), table, ((0,), (0,)))
        lines[0] = mixed[:, 0:128]
        lines[1] = mixed[:, 128:256]
        parts = []
        for low in range(N_LED):
            re, im = (lines[c, pl.ds(low, 8, stride=32)] for c in range(2))
            cos, sin = turn_u[0, low : low + 1], turn_u[1, low : low + 1]
            parts.append((re * cos + im * sin, im * cos - re * sin))
        for part, (re, im) in enumerate(fft_points(parts, -1.0)):
            pr, pi = (pupil[c, part, half * 8 : half * 8 + 8] for c in range(2))
            grad_out[half, part, 0] = pr * re + pi * im
            grad_out[half, part, 1] = pr * im - pi * re
        send_half(led_axis, half, *grad_refs)

    wait_sent(led_axis, *led_refs)
    wait_sent(tile_axis, *tile_refs)
    wait_sent(tile_axis, *back_refs)
    for half in range(2):
        wait_half(led_axis, half, *grad_refs)
        out_ref[half] = grad_in[half]
    wait_sent(led_axis, *grad_refs)


def update_kernel(led_ref, row_ref, col_ref, spec_ref, grad_ref, out_ref):
    led_here = lax.axis_index("led")
    tile_here = lax.axis_index("tile")
    out_ref[...] = spec_ref[...]

    @pl.loop(0, N_LED)
    def _(slot):
        row = window_row(led_ref, row_ref, col_ref, slot, tile_here, led_here)
        for half in range(2):
            for c in range(2):
                span = slice(c * 16 + half * 8, c * 16 + half * 8 + 8)
                out_ref[row, span] = out_ref[row, span] - STEP_SIZE * grad_ref[half, slot, c]


def shards(spectrum, intensities, led_of_slot, row_offset, col_offset, tile_mask, aberration):
    rows = spectrum.reshape(GR * GC, 2 * LINES, 128)
    masks = jnp.transpose(tile_mask, (1, 2, 0)).reshape(64, N_LED)
    smem = pl.BlockSpec(memory_space=pltpu.SMEM)
    vmem = pl.BlockSpec(memory_space=pltpu.VMEM)
    hbm = pl.BlockSpec(memory_space=pltpu.HBM)
    message = pltpu.VMEM((2, N_LED, 2, 8, 128), jnp.float32)
    band = pltpu.VMEM((2, N_TILE, 2, 8, 256), jnp.float32)
    lines = pltpu.VMEM((256, 256), jnp.bfloat16)
    leds = pltpu.SemaphoreType.DMA((2, N_LED))
    tiles = pltpu.SemaphoreType.DMA((2, N_TILE))
    grad = pl.pallas_call(
        exchange_kernel,
        out_shape=jax.ShapeDtypeStruct((2, N_LED, 2, 8, 128), jnp.float32),
        in_specs=[smem] * 5 + [hbm] * 2,
        out_specs=vmem,
        scratch_shapes=[
            pltpu.VMEM((GR * GC, 2 * LINES, 128), jnp.float32),
            pltpu.VMEM((1, BAND, M), jnp.bfloat16),
            pltpu.VMEM((512, 128), jnp.float32),
            lines,
            lines,
            pltpu.VMEM((2, 32, 128), jnp.float32),
            pltpu.VMEM((2, 64, 8, 128), jnp.float32),
            message,
            message,
            pltpu.VMEM((2, N_LED, 16, 128), jnp.float32),
            pltpu.VMEM((2, 256, 128), jnp.float32),
            lines,
            lines,
            band,
            band,
            pltpu.VMEM((2, 4, 16, 8, 128), jnp.float32),
            band,
            band,
            message,
            message,
            pltpu.SemaphoreType.DMA,
            pltpu.SemaphoreType.DMA,
            leds,
            leds,
            tiles,
            tiles,
            tiles,
            tiles,
            leds,
            leds,
        ],
        compiler_params=pltpu.CompilerParams(
            collective_id=0, has_side_effects=True, vmem_limit_bytes=40 * 1024 * 1024
        ),
    )(led_of_slot, row_offset, col_offset, masks, aberration, rows, intensities)
    updated = pl.pallas_call(
        update_kernel,
        out_shape=jax.ShapeDtypeStruct((GR * GC, 2 * LINES, 128), jnp.float32),
        in_specs=[smem] * 3 + [vmem] * 2,
        out_specs=vmem,
        compiler_params=pltpu.CompilerParams(vmem_limit_bytes=24 * 1024 * 1024),
    )(led_of_slot, row_offset, col_offset, rows, grad)
    return updated.reshape(spectrum.shape)


def solution(mesh):
    placed = (P(None, None, "tile", "led", None), P("led", "tile", None), P(), P(), P(), P(), P())
    return jax.shard_map(
        shards,
        mesh=mesh,
        in_specs=placed,
        out_specs=P(None, None, "tile", "led", None),
        check_vma=False,
    )
```

time: 106 us -> 95.7 us (0.903)
  Pallas kernels: 97.9 us -> 89.5 us
  local copies, waits for them, and re-layouts: 7.15 us -> 5.87 us
    pallas_call x2, Pallas kernels: 97.9 us -> 89.5 us  [the longest x1 87.1 us: shards(): pl.pallas_call(exchange_kernel, out_shape=jax.ShapeDtypeStruct((2, N_LED,...]
    unnamed x21 -> x14, local copies, waits for them, and re-layouts: 0.93 us -> 5.87 us
    gather x3 -> x0, local copies, waits for them, and re-layouts: 2.85 us -> none  [arrange_image(): cut = image.reshape(2, 32, 4, 4, 64)[:, :, order][:, :, :, order]]
    convert_element_type x2 -> x0, local copies, waits for them, and re-layouts: 2.08 us -> none  [shards(): image = arrange_image(intensities.reshape(BAND, M)).astype(jnp.float32)]
    another operation x2 -> x0, local copies, waits for them, and re-layouts: 1.19 us -> none  [arrange_image(): cut = image.reshape(2, 32, 4, 4, 64)[:, :, order][:, :, :, order]]
where the time goes in v1:
time: 95.7 us; the launch traced here: 95.4 us
  Pallas kernels  89.5 us (94%)
  local copies, waits for them, and re-layouts  5.87 us (6%)
    pallas_call x1, Pallas kernels, shards(): pl.pallas_call(exchange_kernel, out_shape=jax.ShapeDtypeStruct((2, N_LED,...  87.1 us
    unnamed x14, local copies, waits for them, and re-layouts  5.87 us
    pallas_call x1, Pallas kernels, shards(): pl.pallas_call(update_kernel, out_shape=jax.ShapeDtypeStruct((GR * GC, 2...  2.46 us

profile of v1, /device:TPU:1, one launch (start us, length us, event | category | flops | bytes accessed | tf_op | source)
XLA Modules:
  0.0 95.4 jit_solution(15285538403364958111)
XLA Ops:
  0.0 0.0 copy-start
  0.0 1.6 %copy-done = f32[16,8,1,1,4096]{4,3,2,1,0:T(1,128)S(1)} copy-done((f32[16,8,1,1,4096]{4,3,2,1,0:T(1,128)S(1)}, f32[16,8,1,1,4096]{4,3,2,1,0:T(1,128)}, u32[]{:S(2)}) %copy-start) | copy-done | bytes 2097176
  1.6 0.0 copy-start.1
  1.6 0.9 copy-done.1
  2.5 0.0 copy-start.2
  2.5 0.8 copy-done.2
  3.3 0.0 copy-start.3
  3.3 0.7 copy-done.3
  3.9 0.0 copy-start.4
  3.9 0.7 copy-done.4
  4.6 0.0 copy-start.5
  4.6 0.7 copy-done.5
  5.2 0.0 copy-start.6
  5.2 0.7 copy-done.6
  5.9 87.1 %shard_map.73.grad_ref = f32[2,32,2,8,128]{4,3,2,1,0:T(8,128)S(1)} custom-call(s32[32]{0:T(128)S(1)} %copy-done.3, s32[32]{0:T(128)S(1)} %copy-done.4, s32[32]{0:T(128)S(1)} %copy-done.5, s32[64,32]{1,0:T(8,128)S(1)} %bitcast.7, f32[5]{0:T(128)S(1)} %copy-done.6, f32[128,32,128]{2,1,0:T(8,128)S(1)} %bitcast.5, bf16[1,64,1024]{2,1,0:T(8,128)(2,1)S(1)} %copy-done.1), custom_call_target="tpu_custom_call" | custom-call | tf_op jit(solution)/shard_map/pallas_call | solution.py:404
  93.0 2.5 %shard_map.74 = f32[128,32,128]{2,1,0:T(8,128)} custom-call(s32[32]{0:T(128)S(1)} %copy-done.3, s32[32]{0:T(128)S(1)} %copy-done.4, s32[32]{0:T(128)S(1)} %copy-done.5, f32[128,32,128]{2,1,0:T(8,128)S(1)} %bitcast.6, f32[2,32,2,8,128]{4,3,2,1,0:T(8,128)S(1)} %shard_map.73.grad_ref), custom_call_target="tpu_custom_call" | custom-call | tf_op jit(solution)/shard_map/pallas_call | solution.py:445
Async XLA Ops:
  0.0 1.6 %copy-start = (f32[16,8,1,1,4096]{4,3,2,1,0:T(1,128)S(1)}, f32[16,8,1,1,4096]{4,3,2,1,0:T(1,128)}, u32[]{:S(2)}) copy-start(f32[16,8,1,1,4096]{4,3,2,1,0:T(1,128)} %param.7) | copy-start | bytes 6291460
  1.6 0.9 copy-start.1
  2.5 0.8 copy-start.2
  3.3 0.7 copy-start.3
  3.9 0.7 copy-start.4
  4.6 0.7 copy-start.5
  5.2 0.7 copy-start.6

commit v2 on v1

--- a/solution.py
+++ b/solution.py
@@ -16,6 +16,7 @@
 BAND = M // N_TILE
 CU = M // N_LED
 LINES = BAND * CU // 128
+PARTS = 4
 STEP_SIZE = 0.25
 MESH = pl.DeviceIdType.MESH
 
@@ -127,19 +128,15 @@
 
 
 def exchange_kernel(
-    led_ref, row_ref, col_ref, mask_ref, aber_ref, spec_hbm, image_hbm, out_ref,
-    spec, measured, image, table_hi, table_lo, turn_u, turn_j,
+    led_hbm, row_hbm, col_hbm, mask_hbm, aber_hbm, spec_hbm, image_hbm, grad_hbm,
+    led_ref, row_ref, col_ref, mask_ref, aber_ref, spec, measured,
+    image, table_hi, table_lo, turn_u, turn_j,
     outgoing, window, pupil, lines, lines_hi, lines_lo, bands_out, bands_in, cells, back_out, back_in,
-    grad_out, grad_in, spec_sem, image_sem,
+    grad_out, load_sem, own_sem,
     led_send, led_recv, tile_send, tile_recv, back_send, back_recv, grad_send, grad_recv,
 ):
     led_here = lax.axis_index("led")
     tile_here = lax.axis_index("tile")
-
-    spec_copy = pltpu.make_async_copy(spec_hbm, spec, spec_sem)
-    image_copy = pltpu.make_async_copy(image_hbm, measured, image_sem)
-    spec_copy.start()
-    image_copy.start()
     barrier = pltpu.get_barrier_semaphore()
 
     def far_first(step, count, here):
@@ -151,62 +148,71 @@
         peer = far_first(step, N_LED, led_here)
         pl.semaphore_signal(barrier, inc=1, device_id={"led": peer}, device_id_type=MESH)
 
+    loads = [
+        pltpu.make_async_copy(src, dst, load_sem.at[k])
+        for k, (src, dst) in enumerate(
+            (
+                (led_hbm, led_ref), (row_hbm, row_ref), (col_hbm, col_ref), (mask_hbm, mask_ref),
+                (aber_hbm, aber_ref), (spec_hbm, spec), (image_hbm, measured),
+            )
+        )
+    ]
+    for load in loads:
+        load.start()
+
     @pl.loop(1, N_TILE)
     def _(step):
         peer = far_first(step, N_TILE, tile_here)
         pl.semaphore_signal(barrier, inc=1, device_id={"tile": peer}, device_id_type=MESH)
 
-    def led_copy(src, dst, sends, recvs, half, peer, origin):
+    def target(peer, count, here):
+        return (here + 1) % count if isinstance(peer, pl.Slice) else peer
+
+    def led_copy(src, dst, sends, recvs, part, peer, origin):
         return pltpu.make_async_remote_copy(
-            src_ref=src.at[half, peer], dst_ref=dst.at[half, origin],
-            send_sem=sends.at[half, peer], recv_sem=recvs.at[half, origin],
-            device_id={"led": peer}, device_id_type=MESH,
-        )
-
-    def tile_copy(src, dst, sends, recvs, half, peer, origin):
+            src_ref=src.at[part, peer], dst_ref=dst.at[part, origin],
+            send_sem=sends.at[part], recv_sem=recvs.at[part],
+            device_id={"led": target(peer, N_LED, led_here)}, device_id_type=MESH,
+        )
+
+    def tile_copy(src, dst, sends, recvs, part, peer, origin):
         return pltpu.make_async_remote_copy(
-            src_ref=src.at[half, peer], dst_ref=dst.at[half, origin],
-            send_sem=sends.at[half, peer], recv_sem=recvs.at[half, origin],
-            device_id={"tile": peer}, device_id_type=MESH,
+            src_ref=src.at[part, peer], dst_ref=dst.at[part, origin],
+            send_sem=sends.at[part], recv_sem=recvs.at[part],
+            device_id={"tile": target(peer, N_TILE, tile_here)}, device_id_type=MESH,
         )
 
     led_axis = (led_copy, N_LED, led_here)
     tile_axis = (tile_copy, N_TILE, tile_here)
 
-    def send_half(axis, half, src, dst, sends, recvs):
+    def send_part(axis, part, src, dst, sends, recvs):
         copy, count, here = axis
 
         @pl.loop(1, count)
         def _(step):
-            copy(src, dst, sends, recvs, half, far_first(step, count, here), here).start()
-
-        dst[half, here] = src[half, here]
-
-    def wait_half(axis, half, src, dst, sends, recvs):
+            copy(src, dst, sends, recvs, part, far_first(step, count, here), here).start()
+
+    def all_copies(axis, part, src, dst, sends, recvs):
         copy, count, here = axis
-
-        @pl.loop(1, count)
-        def _(step):
-            peer = far_first(step, count, here)
-            copy(src, dst, sends, recvs, half, peer, peer).wait_recv()
-
-    def wait_sent(axis, src, dst, sends, recvs):
-        copy, count, here = axis
-
-        @pl.loop(1, count)
-        def _(step):
-            peer = far_first(step, count, here)
-            copy(src, dst, sends, recvs, 0, peer, peer).wait_send()
-            copy(src, dst, sends, recvs, 1, peer, peer).wait_send()
-
-    spec_copy.wait()
+        peers = pl.ds(0, count - 1)
+        return copy(src, dst, sends, recvs, part, peers, peers)
+
+    def wait_part(axis, part, *refs):
+        all_copies(axis, part, *refs).wait_recv()
+
+    def wait_sent(axis, *refs):
+        for part in range(PARTS):
+            all_copies(axis, part, *refs).wait_send()
+
+    for load in loads:
+        load.wait()
 
     @pl.loop(0, N_LED)
     def _(slot):
         row = window_row(led_ref, row_ref, col_ref, slot, tile_here, led_here)
-        for half in range(2):
+        for part in range(PARTS):
             for c in range(2):
-                outgoing[half, slot, c] = spec[row, c * 16 + half * 8 : c * 16 + half * 8 + 8]
+                outgoing[part, slot, 4 * c : 4 * c + 4] = spec[row, c * 16 + part * 4 : c * 16 + part * 4 + 4]
 
     def turns(index, modulus):
         return cos_sin((index & (modulus - 1)).astype(jnp.float32) * (2.0 * math.pi / modulus))
@@ -248,8 +254,8 @@
     coord_p = (row_window - M // 2).astype(jnp.float32) * (1.0 / (M // 2))
 
     @pl.loop(0, N_LED)
-    def _(part):
-        col_first = (part * CU - col_start) & (M - 1)
+    def _(origin):
+        col_first = (origin * CU - col_start) & (M - 1)
         coord_q = (col_first + (lane & 31) - M // 2).astype(jnp.float32) * (1.0 / (M // 2))
         radial = coord_p * coord_p + coord_q * coord_q
         phase = (
@@ -261,16 +267,17 @@
         )
         gate = mask_ref[(row_first >> 7) * 8 + (col_first >> 7), led].astype(jnp.float32)
         cos, sin = cos_sin(phase)
-        pupil[0, part] = gate * cos
-        pupil[1, part] = gate * sin
+        for part in range(PARTS):
+            pupil[part, origin, 0:4] = gate * cos[part * 4 : part * 4 + 4]
+            pupil[part, origin, 4:8] = gate * sin[part * 4 : part * 4 + 4]
 
     pl.semaphore_wait(barrier, N_LED + N_TILE - 2)
 
     led_refs = (outgoing, window, led_send, led_recv)
-    send_half(led_axis, 0, *led_refs)
-    send_half(led_axis, 1, *led_refs)
-
-    image_copy.wait()
+    for part in range(PARTS):
+        send_part(led_axis, part, *led_refs)
+        window[part, led_here] = outgoing[part, led_here]
+
     chunk64 = iota((64, 128), 1) >> 5
     for h in range(4):
         pieces = []
@@ -287,34 +294,32 @@
 
     tile_refs = (bands_out, bands_in, tile_send, tile_recv)
     table = (table_hi[...], table_lo[...])
-    for half in range(2):
-        wait_half(led_axis, half, *led_refs)
-        parts = []
-        for part in range(N_LED):
-            pr, pi = (pupil[c, part, half * 8 : half * 8 + 8] for c in range(2))
-            wr, wi = window[half, part, 0], window[half, part, 1]
-            parts.append((pr * wr - pi * wi, pr * wi + pi * wr))
-        for low, (re, im) in enumerate(fft_points(parts, 1.0)):
+    for part in range(PARTS):
+        wait_part(led_axis, part, *led_refs)
+        points = []
+        for origin in range(N_LED):
+            pr, pi = pupil[part, origin, 0:4], pupil[part, origin, 4:8]
+            wr, wi = window[part, origin, 0:4], window[part, origin, 4:8]
+            points.append((pr * wr - pi * wi, pr * wi + pi * wr))
+        for low, (re, im) in enumerate(fft_points(points, 1.0)):
             cos, sin = turn_u[0, low : low + 1], turn_u[1, low : low + 1]
-            lines[0, low * 8 : low * 8 + 8] = re * cos - im * sin
-            lines[1, low * 8 : low * 8 + 8] = im * cos + re * sin
-        for line in range(8):
+            lines[0, low * 4 : low * 4 + 4] = re * cos - im * sin
+            lines[1, low * 4 : low * 4 + 4] = im * cos + re * sin
+        for line in range(4):
             for c in range(2):
-                high, low = halves(lines[c, pl.ds(line, 32, stride=8)])
+                high, low = halves(lines[c, pl.ds(line, 32, stride=4)])
                 lines_hi[line * 32 : line * 32 + 32, c * 128 : c * 128 + 128] = high
                 lines_lo[line * 32 : line * 32 + 32, c * 128 : c * 128 + 128] = low
         mixed = product(table, (lines_hi[...], lines_lo[...]), ((1,), (1,)))
-        bands_out[half] = mixed.reshape(N_TILE, 2, 8, 256)
-        send_half(tile_axis, half, *tile_refs)
-
-    for half in range(2):
-        wait_half(tile_axis, half, *tile_refs)
-        points = fft_points([(bands_in[half, k, 0], bands_in[half, k, 1]) for k in range(N_TILE)], 1.0)
+        bands_out[part] = mixed.reshape(N_TILE, 2, 8, 128)
+        send_part(tile_axis, part, *tile_refs)
+        bands_in[part, tile_here] = bands_out[part, tile_here]
+
+    for part in range(PARTS):
+        wait_part(tile_axis, part, *tile_refs)
+        points = fft_points([(bands_in[part, k, 0], bands_in[part, k, 1]) for k in range(N_TILE)], 1.0)
         for low, (re, im) in enumerate(points):
-            for side in range(2):
-                q = 2 * half + side
-                span = slice(side * 128, side * 128 + 128)
-                cells[0, q, low], cells[1, q, low] = turn(re[:, span], im[:, span], 2.0 * math.pi * low * q / 64)
+            cells[0, part, low], cells[1, part, low] = turn(re, im, 2.0 * math.pi * low * part / 64)
 
     @pl.loop(0, 4)
     def _(chunk):
@@ -341,38 +346,44 @@
             cells[1, q, span] = im
 
     back_refs = (back_out, back_in, back_send, back_recv)
-    for half in range(2):
-        for side in range(2):
-            q = 2 * half + side
-            points = [turn(cells[0, q, low], cells[1, q, low], -2.0 * math.pi * low * q / 64) for low in range(16)]
-            for k, (re, im) in enumerate(fft_points(points, -1.0)):
-                back_out[half, k, 0, :, side * 128 : side * 128 + 128] = re
-                back_out[half, k, 1, :, side * 128 : side * 128 + 128] = im
-        send_half(tile_axis, half, *back_refs)
-
-    grad_refs = (grad_out, grad_in, grad_send, grad_recv)
-    for half in range(2):
-        wait_half(tile_axis, half, *back_refs)
-        mixed = product(halves(back_in[half].reshape(256, 256)), table, ((0,), (0,)))
+    for part in range(PARTS):
+        points = [
+            turn(cells[0, part, low], cells[1, part, low], -2.0 * math.pi * low * part / 64) for low in range(16)
+        ]
+        for k, (re, im) in enumerate(fft_points(points, -1.0)):
+            back_out[part, k, 0] = re
+            back_out[part, k, 1] = im
+        send_part(tile_axis, part, *back_refs)
+        back_in[part, tile_here] = back_out[part, tile_here]
+
+    grad_refs = (grad_out, grad_hbm, grad_send, grad_recv)
+    own = []
+    for part in range(PARTS):
+        wait_part(tile_axis, part, *back_refs)
+        mixed = product(halves(back_in[part].reshape(256, 128)), table, ((0,), (0,)))
         lines[0] = mixed[:, 0:128]
         lines[1] = mixed[:, 128:256]
-        parts = []
+        points = []
         for low in range(N_LED):
-            re, im = (lines[c, pl.ds(low, 8, stride=32)] for c in range(2))
+            re, im = (lines[c, pl.ds(low, 4, stride=32)] for c in range(2))
             cos, sin = turn_u[0, low : low + 1], turn_u[1, low : low + 1]
-            parts.append((re * cos + im * sin, im * cos - re * sin))
-        for part, (re, im) in enumerate(fft_points(parts, -1.0)):
-            pr, pi = (pupil[c, part, half * 8 : half * 8 + 8] for c in range(2))
-            grad_out[half, part, 0] = pr * re + pi * im
-            grad_out[half, part, 1] = pr * im - pi * re
-        send_half(led_axis, half, *grad_refs)
+            points.append((re * cos + im * sin, im * cos - re * sin))
+        for origin, (re, im) in enumerate(fft_points(points, -1.0)):
+            pr, pi = pupil[part, origin, 0:4], pupil[part, origin, 4:8]
+            grad_out[part, origin, 0:4] = pr * re + pi * im
+            grad_out[part, origin, 4:8] = pr * im - pi * re
+        send_part(led_axis, part, *grad_refs)
+        own.append(
+            pltpu.make_async_copy(grad_out.at[part, led_here], grad_hbm.at[part, led_here], own_sem.at[part])
+        )
+        own[-1].start()
 
     wait_sent(led_axis, *led_refs)
     wait_sent(tile_axis, *tile_refs)
     wait_sent(tile_axis, *back_refs)
-    for half in range(2):
-        wait_half(led_axis, half, *grad_refs)
-        out_ref[half] = grad_in[half]
+    for part in range(PARTS):
+        own[part].wait()
+        wait_part(led_axis, part, *grad_refs)
     wait_sent(led_axis, *grad_refs)
 
 
@@ -380,14 +391,18 @@
     led_here = lax.axis_index("led")
     tile_here = lax.axis_index("tile")
     out_ref[...] = spec_ref[...]
+    low = lax.broadcasted_iota(jnp.int32, (8, 128), 0) < 4
 
     @pl.loop(0, N_LED)
     def _(slot):
         row = window_row(led_ref, row_ref, col_ref, slot, tile_here, led_here)
         for half in range(2):
-            for c in range(2):
+            first, second = grad_ref[2 * half, slot], grad_ref[2 * half + 1, slot]
+            re = jnp.where(low, first, pltpu.roll(second, 4, 0))
+            im = jnp.where(low, pltpu.roll(first, 4, 0), second)
+            for c, step in ((0, re), (1, im)):
                 span = slice(c * 16 + half * 8, c * 16 + half * 8 + 8)
-                out_ref[row, span] = out_ref[row, span] - STEP_SIZE * grad_ref[half, slot, c]
+                out_ref[row, span] = out_ref[row, span] - STEP_SIZE * step
 
 
 def shards(spectrum, intensities, led_of_slot, row_offset, col_offset, tile_mask, aberration):
@@ -396,50 +411,47 @@
     smem = pl.BlockSpec(memory_space=pltpu.SMEM)
     vmem = pl.BlockSpec(memory_space=pltpu.VMEM)
     hbm = pl.BlockSpec(memory_space=pltpu.HBM)
-    message = pltpu.VMEM((2, N_LED, 2, 8, 128), jnp.float32)
-    band = pltpu.VMEM((2, N_TILE, 2, 8, 256), jnp.float32)
-    lines = pltpu.VMEM((256, 256), jnp.bfloat16)
-    leds = pltpu.SemaphoreType.DMA((2, N_LED))
-    tiles = pltpu.SemaphoreType.DMA((2, N_TILE))
+    message = pltpu.VMEM((PARTS, N_LED, 8, 128), jnp.float32)
+    band = pltpu.VMEM((PARTS, N_TILE, 2, 8, 128), jnp.float32)
+    table = pltpu.VMEM((256, 256), jnp.bfloat16)
+    lines = pltpu.VMEM((128, 256), jnp.bfloat16)
+    sems = pltpu.SemaphoreType.DMA((PARTS,))
     grad = pl.pallas_call(
         exchange_kernel,
-        out_shape=jax.ShapeDtypeStruct((2, N_LED, 2, 8, 128), jnp.float32),
-        in_specs=[smem] * 5 + [hbm] * 2,
-        out_specs=vmem,
+        out_shape=jax.ShapeDtypeStruct((PARTS, N_LED, 8, 128), jnp.float32),
+        in_specs=[hbm] * 7,
+        out_specs=hbm,
         scratch_shapes=[
+            pltpu.SMEM((N_LED,), jnp.int32),
+            pltpu.SMEM((N_LED,), jnp.int32),
+            pltpu.SMEM((N_LED,), jnp.int32),
+            pltpu.SMEM((64, N_LED), jnp.int32),
+            pltpu.SMEM((5,), jnp.float32),
             pltpu.VMEM((GR * GC, 2 * LINES, 128), jnp.float32),
             pltpu.VMEM((1, BAND, M), jnp.bfloat16),
             pltpu.VMEM((512, 128), jnp.float32),
-            lines,
-            lines,
+            table,
+            table,
             pltpu.VMEM((2, 32, 128), jnp.float32),
             pltpu.VMEM((2, 64, 8, 128), jnp.float32),
             message,
             message,
-            pltpu.VMEM((2, N_LED, 16, 128), jnp.float32),
-            pltpu.VMEM((2, 256, 128), jnp.float32),
+            message,
+            pltpu.VMEM((2, 128, 128), jnp.float32),
             lines,
             lines,
             band,
             band,
-            pltpu.VMEM((2, 4, 16, 8, 128), jnp.float32),
+            pltpu.VMEM((2, PARTS, 16, 8, 128), jnp.float32),
             band,
             band,
             message,
-            message,
-            pltpu.SemaphoreType.DMA,
-            pltpu.SemaphoreType.DMA,
-            leds,
-            leds,
-            tiles,
-            tiles,
-            tiles,
-            tiles,
-            leds,
-            leds,
-        ],
+            pltpu.SemaphoreType.DMA((7,)),
+            pltpu.SemaphoreType.DMA((PARTS,)),
+        ]
+        + [sems] * 8,
         compiler_params=pltpu.CompilerParams(
-            collective_id=0, has_side_effects=True, vmem_limit_bytes=40 * 1024 * 1024
+            collective_id=0, has_side_effects=True, vmem_limit_bytes=60 * 1024 * 1024
         ),
     )(led_of_slot, row_offset, col_offset, masks, aberration, rows, intensities)
     updated = pl.pallas_call(
@@ -447,7 +459,7 @@
         out_shape=jax.ShapeDtypeStruct((GR * GC, 2 * LINES, 128), jnp.float32),
         in_specs=[smem] * 3 + [vmem] * 2,
         out_specs=vmem,
-        compiler_params=pltpu.CompilerParams(vmem_limit_bytes=24 * 1024 * 1024),
+        compiler_params=pltpu.CompilerParams(vmem_limit_bytes=60 * 1024 * 1024),
     )(led_of_slot, row_offset, col_offset, rows, grad)
     return updated.reshape(spectrum.shape)
 

time: 95.7 us -> 84.9 us (0.89)
  local copies, waits for them, and re-layouts: 5.87 us -> 0 us
  Pallas kernels: 89.5 us -> 84.7 us
    pallas_call x1, Pallas kernels: 87.1 us -> 81.1 us  [shards(): pl.pallas_call(exchange_kernel, out_shape=jax.ShapeDtypeStruct((PARTS, N_...]
    unnamed x14 -> x0, local copies, waits for them, and re-layouts: 5.87 us -> none
    pallas_call x1, Pallas kernels: 2.46 us -> 3.6 us  [shards(): pl.pallas_call(update_kernel, out_shape=jax.ShapeDtypeStruct((GR * GC, 2...]
where the time goes in v2:
time: 84.9 us; the launch traced here: 84.7 us
  Pallas kernels  84.7 us (100%)
    pallas_call x1, Pallas kernels, shards(): pl.pallas_call(exchange_kernel, out_shape=jax.ShapeDtypeStruct((PARTS, N_...  81.1 us
    pallas_call x1, Pallas kernels, shards(): pl.pallas_call(update_kernel, out_shape=jax.ShapeDtypeStruct((GR * GC, 2...  3.6 us

profile of v2, /device:TPU:1, one launch (start us, length us, event | category | flops | bytes accessed | tf_op | source)
XLA Modules:
  0.0 84.7 jit_solution(16448028465782830251)
XLA Ops:
  0.0 81.1 %shard_map.73.grad_ref = f32[4,32,8,128]{3,2,1,0:T(8,128)} custom-call(s32[32]{0:T(128)} %led_ref.1, s32[32]{0:T(128)} %row_ref.1, s32[32]{0:T(128)} %col_ref.1, s32[64,32]{1,0:T(8,128)} %bitcast.7, f32[5]{0:T(128)} %aber_hbm.1, f32[128,32,128]{2,1,0:T(8,128)} %bitcast.5, bf16[1,64,1024]{2,1,0:T(8,128)(2,1)} %image_hbm.1), custom_call_target="tpu_custom_call" | custom-call | tf_op jit(solution)/shard_map/pallas_call | solution.py:419
  81.1 3.6 %shard_map.74 = f32[128,32,128]{2,1,0:T(8,128)} custom-call(s32[32]{0:T(128)} %led_ref.1, s32[32]{0:T(128)} %row_ref.1, s32[32]{0:T(128)} %col_ref.1, f32[128,32,128]{2,1,0:T(8,128)} %bitcast.6, f32[4,32,8,128]{3,2,1,0:T(8,128)} %shard_map.73.grad_ref), custom_call_target="tpu_custom_call" | custom-call | tf_op jit(solution)/shard_map/pallas_call | solution.py:457

commit v3 on v2

--- a/solution.py
+++ b/solution.py
@@ -57,35 +57,24 @@
     return out
 
 
-def digit(shape, axis, unit):
-    return lax.broadcasted_iota(jnp.int32, shape, axis) // unit
-
-
-def swapped(x, distance, axis):
-    size = x.shape[axis]
-    if 2 * distance == size:
-        return pltpu.roll(x, distance, axis)
-    low = digit(x.shape, axis, distance) % 2 == 0
-    return jnp.where(low, pltpu.roll(x, size - distance, axis), pltpu.roll(x, distance, axis))
-
-
-def four_forward(re, im, axis, unit):
-    group = digit(re.shape, axis, unit)
-    first = jnp.where(group < 2, 1.0, -1.0)
-    second = jnp.where(group % 2 == 0, 1.0, -1.0)
-    re = first * re + swapped(re, 2 * unit, axis)
-    im = first * im + swapped(im, 2 * unit, axis)
-    re, im = jnp.where(group == 3, -im, re), jnp.where(group == 3, re, im)
-    return second * re + swapped(re, unit, axis), second * im + swapped(im, unit, axis)
-
-
-def four_backward(re, im, axis, unit):
-    group = digit(re.shape, axis, unit)
-    first = jnp.where(group < 2, 1.0, -1.0)
-    second = jnp.where(group % 2 == 0, 1.0, -1.0)
-    re, im = second * re + swapped(re, unit, axis), second * im + swapped(im, unit, axis)
-    re, im = jnp.where(group == 3, im, re), jnp.where(group == 3, -re, im)
-    return first * re + swapped(re, 2 * unit, axis), first * im + swapped(im, 2 * unit, axis)
+def trade_bit(parts, bit, axis, unit):
+    size = parts[0].shape[axis]
+    clear = (lax.broadcasted_iota(jnp.int32, parts[0].shape, axis) // unit) % 2 == 0
+    out = list(parts)
+    for low in range(len(parts)):
+        if low & bit == 0:
+            a, b = parts[low], parts[low | bit]
+            out[low] = jnp.where(clear, a, pltpu.roll(b, unit, axis))
+            out[low | bit] = jnp.where(clear, pltpu.roll(a, size - unit, axis), b)
+    return out
+
+
+def trade(points, axis, unit):
+    halves_here = []
+    for parts in zip(*points):
+        parts = trade_bit(list(parts), 2, axis, 2 * unit)
+        halves_here.append(trade_bit(parts, 1, axis, unit))
+    return list(zip(*halves_here))
 
 
 def cos_sin(phase):
@@ -214,6 +203,13 @@
             for c in range(2):
                 outgoing[part, slot, 4 * c : 4 * c + 4] = spec[row, c * 16 + part * 4 : c * 16 + part * 4 + 4]
 
+    pl.semaphore_wait(barrier, N_LED + N_TILE - 2)
+
+    led_refs = (outgoing, window, led_send, led_recv)
+    for part in range(PARTS):
+        send_part(led_axis, part, *led_refs)
+        window[part, led_here] = outgoing[part, led_here]
+
     def turns(index, modulus):
         return cos_sin((index & (modulus - 1)).astype(jnp.float32) * (2.0 * math.pi / modulus))
 
@@ -241,9 +237,7 @@
     def _(low):
         turn_j[0, low], turn_j[1, low] = turns(low * (4 * (lane8 >> 5) + (sub8 >> 1)), M)
 
-    chunk8 = lane8 >> 5
-    frequency8 = jnp.where(chunk8 == 1, 2, jnp.where(chunk8 == 2, 1, chunk8))
-    turn_hr, turn_hi = turns((sub8 >> 1) * frequency8, 16)
+    turn_h = [turns((sub8 >> 1) * f, 16) for f in range(4)]
 
     led = led_ref[led_here]
     row_start = row_ref[led] * TILE
@@ -271,26 +265,19 @@
             pupil[part, origin, 0:4] = gate * cos[part * 4 : part * 4 + 4]
             pupil[part, origin, 4:8] = gate * sin[part * 4 : part * 4 + 4]
 
-    pl.semaphore_wait(barrier, N_LED + N_TILE - 2)
-
-    led_refs = (outgoing, window, led_send, led_recv)
-    for part in range(PARTS):
-        send_part(led_axis, part, *led_refs)
-        window[part, led_here] = outgoing[part, led_here]
-
-    chunk64 = iota((64, 128), 1) >> 5
-    for h in range(4):
-        pieces = []
-        for block in (2 * h, 2 * h + 1):
-            lines_here = measured[0, :, block * 128 : block * 128 + 128].astype(jnp.float32)
-            turned = jnp.transpose(jnp.concatenate([lines_here, lines_here], axis=0))
-            rolled = pltpu.roll(turned, 32, 1)
-            pieces += [(turned[f : f + 64], rolled[f : f + 64]) for f in (0, 64)]
-        for s in range(2):
-            merged = pieces[0][s]
-            for m, f in ((1, 2), (2, 1), (3, 3)):
-                merged = jnp.where(chunk64 == m, pieces[f][(m + s) % 2], merged)
-            image[pl.ds((0, 2, 1, 3)[h] * 2 + s, 64, stride=8), :] = merged
+    chunk16 = iota((16, 128), 1) >> 5
+    for block in range(8):
+        lines_here = measured[0, :, block * 128 : block * 128 + 128].astype(jnp.float32)
+        turned = jnp.transpose(jnp.concatenate([lines_here, lines_here], axis=0))
+        sides = (turned, pltpu.roll(turned, 32, 1))
+        for odd in range(2):
+            f = 2 * (block % 2) + odd
+            for s in range(2):
+                pieces = [sides[(g + s) % 2][odd * 64 + g * 16 : odd * 64 + g * 16 + 16] for g in range(4)]
+                merged = pieces[0]
+                for g in range(1, 4):
+                    merged = jnp.where(chunk16 == g, pieces[g], merged)
+                image[pl.ds((block // 2) * 128 + 2 * f + s, 16, stride=8), :] = merged
 
     tile_refs = (bands_out, bands_in, tile_send, tile_recv)
     table = (table_hi[...], table_lo[...])
@@ -324,24 +311,22 @@
     @pl.loop(0, 4)
     def _(chunk):
         span = pl.ds(chunk * 4, 4)
-        quads = fft_points([(cells[0, q, span], cells[1, q, span]) for q in range(4)], 1.0)
-        back = []
-        for q, (re, im) in enumerate(quads):
-            where = pl.ds(16 * q + chunk * 4, 4)
-            jr, ji = turn_j[0, where], turn_j[1, where]
-            hr, hi = turn_hr[None], turn_hi[None]
-            re, im = re * jr - im * ji, im * jr + re * ji
-            re, im = four_forward(re, im, 2, 32)
-            re, im = re * hr - im * hi, im * hr + re * hi
-            re, im = four_forward(re, im, 1, 2)
-            seen = image[pl.ds(pl.multiple_of((16 * q + chunk * 4) * 8, 32), 32), :].reshape(4, 8, 128)
-            excess = re * re + im * im - seen
-            re, im = excess * re, excess * im
-            re, im = four_backward(re, im, 1, 2)
-            re, im = re * hr + im * hi, im * hr - re * hi
-            re, im = four_backward(re, im, 2, 32)
-            back.append((re * jr + im * ji, im * jr - re * ji))
-        for q, (re, im) in enumerate(fft_points(back, -1.0)):
+        tables = [(turn_j[0, where], turn_j[1, where]) for where in (pl.ds(16 * g + chunk * 4, 4) for g in range(4))]
+        points = fft_points([(cells[0, q, span], cells[1, q, span]) for q in range(4)], 1.0)
+        points = [(re * c - im * s, im * c + re * s) for (re, im), (c, s) in zip(points, tables)]
+        points = fft_points(trade(points, 2, 32), 1.0)
+        points = [(re * c - im * s, im * c + re * s) for (re, im), (c, s) in zip(points, turn_h)]
+        points = fft_points(trade(points, 1, 2), 1.0)
+        excess = []
+        for h, (re, im) in enumerate(points):
+            start = pl.multiple_of((16 * h + chunk * 4) * 8, 32)
+            rest = re * re + im * im - image[pl.ds(start, 32), :].reshape(4, 8, 128)
+            excess.append((rest * re, rest * im))
+        points = trade(fft_points(excess, -1.0), 1, 2)
+        points = [(re * c + im * s, im * c - re * s) for (re, im), (c, s) in zip(points, turn_h)]
+        points = trade(fft_points(points, -1.0), 2, 32)
+        points = [(re * c + im * s, im * c - re * s) for (re, im), (c, s) in zip(points, tables)]
+        for q, (re, im) in enumerate(fft_points(points, -1.0)):
             cells[0, q, span] = re
             cells[1, q, span] = im
 
@@ -387,29 +372,58 @@
     wait_sent(led_axis, *grad_refs)
 
 
-def update_kernel(led_ref, row_ref, col_ref, spec_ref, grad_ref, out_ref):
+def update_kernel(
+    led_hbm, row_hbm, col_hbm, spec_hbm, grad_hbm, out_hbm, led_ref, row_ref, col_ref, rows_ref, spec, grad,
+    load_sem, store_sem,
+):
     led_here = lax.axis_index("led")
     tile_here = lax.axis_index("tile")
-    out_ref[...] = spec_ref[...]
+    sides = [pl.ds(c * 16, 16) for c in range(2)]
+    loads = [
+        pltpu.make_async_copy(src, dst, load_sem.at[k])
+        for k, (src, dst) in enumerate(
+            (
+                (led_hbm, led_ref), (row_hbm, row_ref), (col_hbm, col_ref), (grad_hbm, grad),
+                (spec_hbm.at[:, sides[0]], spec.at[:, sides[0]]), (spec_hbm.at[:, sides[1]], spec.at[:, sides[1]]),
+            )
+        )
+    ]
+    for load in loads:
+        load.start()
+    for load in loads[:3]:
+        load.wait()
+
+    @pl.loop(0, N_LED, unroll=4)
+    def _(slot):
+        rows_ref[slot] = window_row(led_ref, row_ref, col_ref, slot, tile_here, led_here)
+
+    loads[3].wait()
     low = lax.broadcasted_iota(jnp.int32, (8, 128), 0) < 4
-
-    @pl.loop(0, N_LED)
-    def _(slot):
-        row = window_row(led_ref, row_ref, col_ref, slot, tile_here, led_here)
-        for half in range(2):
-            first, second = grad_ref[2 * half, slot], grad_ref[2 * half + 1, slot]
-            re = jnp.where(low, first, pltpu.roll(second, 4, 0))
-            im = jnp.where(low, pltpu.roll(first, 4, 0), second)
-            for c, step in ((0, re), (1, im)):
+    stores = []
+    for c in range(2):
+        loads[4 + c].wait()
+
+        @pl.loop(0, N_LED, unroll=8)
+        def _(slot):
+            row = rows_ref[slot]
+            for half in range(2):
+                first, second = grad[2 * half, slot], grad[2 * half + 1, slot]
+                if c == 0:
+                    step = jnp.where(low, first, pltpu.roll(second, 4, 0))
+                else:
+                    step = jnp.where(low, pltpu.roll(first, 4, 0), second)
                 span = slice(c * 16 + half * 8, c * 16 + half * 8 + 8)
-                out_ref[row, span] = out_ref[row, span] - STEP_SIZE * step
+                spec[row, span] = spec[row, span] - STEP_SIZE * step
+
+        stores.append(pltpu.make_async_copy(spec.at[:, sides[c]], out_hbm.at[:, sides[c]], store_sem.at[c]))
+        stores[c].start()
+    for store in stores:
+        store.wait()
 
 
 def shards(spectrum, intensities, led_of_slot, row_offset, col_offset, tile_mask, aberration):
     rows = spectrum.reshape(GR * GC, 2 * LINES, 128)
     masks = jnp.transpose(tile_mask, (1, 2, 0)).reshape(64, N_LED)
-    smem = pl.BlockSpec(memory_space=pltpu.SMEM)
-    vmem = pl.BlockSpec(memory_space=pltpu.VMEM)
     hbm = pl.BlockSpec(memory_space=pltpu.HBM)
     message = pltpu.VMEM((PARTS, N_LED, 8, 128), jnp.float32)
     band = pltpu.VMEM((PARTS, N_TILE, 2, 8, 128), jnp.float32)
@@ -457,8 +471,18 @@
     updated = pl.pallas_call(
         update_kernel,
         out_shape=jax.ShapeDtypeStruct((GR * GC, 2 * LINES, 128), jnp.float32),
-        in_specs=[smem] * 3 + [vmem] * 2,
-        out_specs=vmem,
+        in_specs=[hbm] * 5,
+        out_specs=hbm,
+        scratch_shapes=[
+            pltpu.SMEM((N_LED,), jnp.int32),
+            pltpu.SMEM((N_LED,), jnp.int32),
+            pltpu.SMEM((N_LED,), jnp.int32),
+            pltpu.SMEM((N_LED,), jnp.int32),
+            pltpu.VMEM((GR * GC, 2 * LINES, 128), jnp.float32),
+            message,
+            pltpu.SemaphoreType.DMA((6,)),
+            pltpu.SemaphoreType.DMA((2,)),
+        ],
         compiler_params=pltpu.CompilerParams(vmem_limit_bytes=60 * 1024 * 1024),
     )(led_of_slot, row_offset, col_offset, rows, grad)
     return updated.reshape(spectrum.shape)

time: 84.9 us -> 83.8 us (0.987)
  Pallas kernels: 84.7 us -> 83.7 us
where the time goes in v3:
time: 83.8 us; the launch traced here: 83.7 us
  Pallas kernels  83.7 us (100%)
    pallas_call x1, Pallas kernels, shards(): pl.pallas_call(exchange_kernel, out_shape=jax.ShapeDtypeStruct((PARTS, N_...  80.8 us
    pallas_call x1, Pallas kernels, shards(): pl.pallas_call(update_kernel, out_shape=jax.ShapeDtypeStruct((GR * GC, 2...  2.89 us

profile of v3, /device:TPU:1, one launch (start us, length us, event | category | flops | bytes accessed | tf_op | source)
XLA Modules:
  0.0 83.7 jit_solution(11964741677973370844)
XLA Ops:
  0.0 80.8 %shard_map.73.grad_hbm = f32[4,32,8,128]{3,2,1,0:T(8,128)} custom-call(s32[32]{0:T(128)} %led_hbm.3, s32[32]{0:T(128)} %row_hbm.3, s32[32]{0:T(128)} %col_hbm.3, s32[64,32]{1,0:T(8,128)} %bitcast.7, f32[5]{0:T(128)} %aber_hbm.1, f32[128,32,128]{2,1,0:T(8,128)} %bitcast.5, bf16[1,64,1024]{2,1,0:T(8,128)(2,1)} %image_hbm.1), custom_call_target="tpu_custom_call" | custom-call | tf_op jit(solution)/shard_map/pallas_call | solution.py:433
  80.8 2.9 %shard_map.74 = f32[128,32,128]{2,1,0:T(8,128)} custom-call(s32[32]{0:T(128)} %led_hbm.3, s32[32]{0:T(128)} %row_hbm.3, s32[32]{0:T(128)} %col_hbm.3, f32[128,32,128]{2,1,0:T(8,128)} %bitcast.6, f32[4,32,8,128]{3,2,1,0:T(8,128)} %shard_map.73.grad_hbm), custom_call_target="tpu_custom_call" | custom-call | tf_op jit(solution)/shard_map/pallas_call | solution.py:471

commit v4 on v3

--- a/solution.py
+++ b/solution.py
@@ -373,49 +373,48 @@
 
 
 def update_kernel(
-    led_hbm, row_hbm, col_hbm, spec_hbm, grad_hbm, out_hbm, led_ref, row_ref, col_ref, rows_ref, spec, grad,
+    led_any, row_any, col_any, spec_ref, grad_hbm, out_hbm, led_ref, row_ref, col_ref, rows_ref, work, grad_ref,
     load_sem, store_sem,
 ):
     led_here = lax.axis_index("led")
     tile_here = lax.axis_index("tile")
-    sides = [pl.ds(c * 16, 16) for c in range(2)]
     loads = [
         pltpu.make_async_copy(src, dst, load_sem.at[k])
         for k, (src, dst) in enumerate(
-            (
-                (led_hbm, led_ref), (row_hbm, row_ref), (col_hbm, col_ref), (grad_hbm, grad),
-                (spec_hbm.at[:, sides[0]], spec.at[:, sides[0]]), (spec_hbm.at[:, sides[1]], spec.at[:, sides[1]]),
-            )
+            ((grad_hbm, grad_ref), (led_any, led_ref), (row_any, row_ref), (col_any, col_ref))
         )
     ]
     for load in loads:
         load.start()
-    for load in loads[:3]:
+    work[:, 0:16] = spec_ref[:, 0:16]
+    for load in loads[1:]:
         load.wait()
 
     @pl.loop(0, N_LED, unroll=4)
     def _(slot):
         rows_ref[slot] = window_row(led_ref, row_ref, col_ref, slot, tile_here, led_here)
 
-    loads[3].wait()
+    loads[0].wait()
     low = lax.broadcasted_iota(jnp.int32, (8, 128), 0) < 4
     stores = []
     for c in range(2):
-        loads[4 + c].wait()
+        if c == 1:
+            work[:, 16:32] = spec_ref[:, 16:32]
 
         @pl.loop(0, N_LED, unroll=8)
         def _(slot):
             row = rows_ref[slot]
             for half in range(2):
-                first, second = grad[2 * half, slot], grad[2 * half + 1, slot]
+                first, second = grad_ref[2 * half, slot], grad_ref[2 * half + 1, slot]
                 if c == 0:
                     step = jnp.where(low, first, pltpu.roll(second, 4, 0))
                 else:
                     step = jnp.where(low, pltpu.roll(first, 4, 0), second)
                 span = slice(c * 16 + half * 8, c * 16 + half * 8 + 8)
-                spec[row, span] = spec[row, span] - STEP_SIZE * step
-
-        stores.append(pltpu.make_async_copy(spec.at[:, sides[c]], out_hbm.at[:, sides[c]], store_sem.at[c]))
+                work[row, span] = work[row, span] - STEP_SIZE * step
+
+        side = pl.ds(c * 16, 16)
+        stores.append(pltpu.make_async_copy(work.at[:, side], out_hbm.at[:, side], store_sem.at[c]))
         stores[c].start()
     for store in stores:
         store.wait()
@@ -425,6 +424,7 @@
     rows = spectrum.reshape(GR * GC, 2 * LINES, 128)
     masks = jnp.transpose(tile_mask, (1, 2, 0)).reshape(64, N_LED)
     hbm = pl.BlockSpec(memory_space=pltpu.HBM)
+    vmem = pl.BlockSpec(memory_space=pltpu.VMEM)
     message = pltpu.VMEM((PARTS, N_LED, 8, 128), jnp.float32)
     band = pltpu.VMEM((PARTS, N_TILE, 2, 8, 128), jnp.float32)
     table = pltpu.VMEM((256, 256), jnp.bfloat16)
@@ -465,13 +465,13 @@
         ]
         + [sems] * 8,
         compiler_params=pltpu.CompilerParams(
-            collective_id=0, has_side_effects=True, vmem_limit_bytes=60 * 1024 * 1024
+            collective_id=0, has_side_effects=True, vmem_limit_bytes=56 * 1024 * 1024
         ),
-    )(led_of_slot, row_offset, col_offset, masks, aberration, rows, intensities)
+    )(*(pltpu.with_memory_space_constraint(x, pltpu.HBM) for x in (led_of_slot, row_offset, col_offset, masks, aberration, rows, intensities)))
     updated = pl.pallas_call(
         update_kernel,
         out_shape=jax.ShapeDtypeStruct((GR * GC, 2 * LINES, 128), jnp.float32),
-        in_specs=[hbm] * 5,
+        in_specs=[pl.BlockSpec(memory_space=pl.ANY)] * 3 + [vmem, hbm],
         out_specs=hbm,
         scratch_shapes=[
             pltpu.SMEM((N_LED,), jnp.int32),
@@ -480,11 +480,11 @@
             pltpu.SMEM((N_LED,), jnp.int32),
             pltpu.VMEM((GR * GC, 2 * LINES, 128), jnp.float32),
             message,
-            pltpu.SemaphoreType.DMA((6,)),
+            pltpu.SemaphoreType.DMA((4,)),
             pltpu.SemaphoreType.DMA((2,)),
         ],
-        compiler_params=pltpu.CompilerParams(vmem_limit_bytes=60 * 1024 * 1024),
-    )(led_of_slot, row_offset, col_offset, rows, grad)
+        compiler_params=pltpu.CompilerParams(vmem_limit_bytes=8 * 1024 * 1024),
+    )(led_of_slot, row_offset, col_offset, rows, pltpu.with_memory_space_constraint(grad, pltpu.HBM))
     return updated.reshape(spectrum.shape)
 
 

time: 83.8 us -> 83.7 us (level)
  no operation moved by 1% of the time
where the time goes in v4:
time: 83.7 us; the launch traced here: 83.5 us
  Pallas kernels  83.4 us (100%)
    pallas_call x1, Pallas kernels, shards(): pl.pallas_call(exchange_kernel, out_shape=jax.ShapeDtypeStruct((PARTS, N_...  80.9 us
    pallas_call x1, Pallas kernels, shards(): pl.pallas_call(update_kernel, out_shape=jax.ShapeDtypeStruct((GR * GC, 2...  2.53 us

profile of v4, /device:TPU:1, one launch (start us, length us, event | category | flops | bytes accessed | tf_op | source)
XLA Modules:
  0.0 83.5 jit_solution(9075206864907896102)
XLA Ops:
  0.0 0.0 copy-start.3
  0.0 0.0 copy-start.2
  0.0 0.0 copy-start.1
  0.0 0.0 copy-start
  0.0 80.9 %shard_map.73.grad_hbm = f32[4,32,8,128]{3,2,1,0:T(8,128)} custom-call(s32[32]{0:T(128)} %led_any.1, s32[32]{0:T(128)} %row_any.1, s32[32]{0:T(128)} %col_any.1, s32[64,32]{1,0:T(8,128)} %bitcast.7, f32[5]{0:T(128)} %aber_hbm.1, f32[128,32,128]{2,1,0:T(8,128)} %bitcast.5, bf16[1,64,1024]{2,1,0:T(8,128)(2,1)} %image_hbm.1), custom_call_target="tpu_custom_call" | custom-call | tf_op jit(solution)/shard_map/pallas_call | solution.py:433
  80.9 0.0 copy-done.3
  80.9 0.0 copy-done.2
  80.9 0.0 copy-done.1
  80.9 0.0 copy-done
  80.9 2.5 %shard_map.74 = f32[128,32,128]{2,1,0:T(8,128)} custom-call(s32[32]{0:T(128)S(1)} %copy-done.1, s32[32]{0:T(128)S(1)} %copy-done.2, s32[32]{0:T(128)S(1)} %copy-done.3, f32[128,32,128]{2,1,0:T(8,128)S(1)} %bitcast.6, f32[4,32,8,128]{3,2,1,0:T(8,128)} %shard_map.73.grad_hbm), custom_call_target="tpu_custom_call" | custom-call | tf_op jit(solution)/shard_map/pallas_call | solution.py:471
Async XLA Ops:
  0.0 80.9 %copy-start.3 = (s32[32]{0:T(128)S(1)}, s32[32]{0:T(128)}, u32[]{:S(2)}) copy-start(s32[32]{0:T(128)} %col_any.1) | copy-start | bytes 388
  0.0 80.9 %copy-start.2 = (s32[32]{0:T(128)S(1)}, s32[32]{0:T(128)}, u32[]{:S(2)}) copy-start(s32[32]{0:T(128)} %row_any.1) | copy-start | bytes 388
  0.0 80.9 %copy-start.1 = (s32[32]{0:T(128)S(1)}, s32[32]{0:T(128)}, u32[]{:S(2)}) copy-start(s32[32]{0:T(128)} %led_any.1) | copy-start | bytes 388
  0.0 80.9 %copy-start = (f32[16,8,1,1,4096]{4,3,2,1,0:T(1,128)S(1)}, f32[16,8,1,1,4096]{4,3,2,1,0:T(1,128)}, u32[]{:S(2)}) copy-start(f32[16,8,1,1,4096]{4,3,2,1,0:T(1,128)} %param.7) | copy-start | bytes 6291460
